TPU v7x, 512 devices: a whole 4x8x8 slice. The times are simulated.
512 devices in a mesh: dp: 4 (over y_hi), seq: 128 (over y_lo, x, z, core).
Axes of the slice: x: 4, y: 8 (y_hi: 4, y_lo: 2; y = y_hi * 2 + y_lo), z: 8, core: 2. Of those that a mesh axis runs over, the one named last changes fastest.
Arguments:
- queries: bfloat16 [4, 16384, 512], P('dp', 'seq'), may hold values from -6 to 6
- key_rows: bfloat16 [4, 16384, 512], P('dp', 'seq'), may hold values from -6 to 6
- value_rows: bfloat16 [4, 16384, 512], P('dp', 'seq'), may hold values from -6 to 6
- out_grad: bfloat16 [4, 16384, 1024], P('dp', 'seq'), may hold values from -6 to 6
- out_weight: bfloat16 [512, 1024], P('seq'), may hold values from -0.25 to 0.25
- norm_gain: float32 [256], replicated, may hold values from 0.1 to 1.9
Outputs:
- query_grad: bfloat16 [4, 16384, 512], P('dp', 'seq')
- key_grad: bfloat16 [4, 16384, 512], P('dp', 'seq')
- value_grad: bfloat16 [4, 16384, 512], P('dp', 'seq')
- weight_grad: float32 [512, 1024], P('seq')
All inputs are finite; a program needn't handle non-finite values.
Results may differ from a plain program's by a relative error of at most 0.025.
Values may be sent and summed in bfloat16 or wider, within the bound.
A program may use at most 64 MiB of HBM per device.

v0:
```python
import math

import jax
import jax.numpy as jnp
from jax import lax
from jax.experimental import pallas as pl
from jax.experimental.pallas import tpu as pltpu
from jax.sharding import PartitionSpec as P

MESH = pl.DeviceIdType.MESH
DH = 128
ROWS = 128
SOFT = 256
N_SEQ = 128
N_DP = 4
norm_eps = 1e-06
BF16 = jnp.bfloat16
F32 = jnp.float32
FAR = (4, 3, 5, 2, 6, 1, 7)


def dot(a, b, a_dim, b_dim):
    return lax.dot_general(a, b, (((a_dim,), (b_dim,)), ((), ())), preferred_element_type=F32)


def parts(x):
    high = x.astype(BF16)
    return high, (x - high.astype(F32)).astype(BF16)


def dot_wide(a, b, a_dim, b_dim):
    if b.dtype == BF16:
        high, low = parts(a)
        return dot(high, b, a_dim, b_dim) + dot(low, b, a_dim, b_dim)
    if a.dtype == BF16:
        high, low = parts(b)
        return dot(a, high, a_dim, b_dim) + dot(a, low, a_dim, b_dim)
    a_high, a_low = parts(a)
    b_high, b_low = parts(b)
    return (
        dot(a_high, b_high, a_dim, b_dim)
        + dot(a_high, b_low, a_dim, b_dim)
        + dot(a_low, b_high, a_dim, b_dim)
    )


def unit_plus(x):
    return jnp.where(x > 0, x + 1.0, jnp.exp(jnp.minimum(x, 0.0)))


def unit_slope(x):
    return jnp.where(x > 0, 1.0, jnp.exp(jnp.minimum(x, 0.0)))


def head(h):
    return slice(h * DH, (h + 1) * DH)


def kernel(
    q_hbm, k_hbm, v_hbm, g_hbm, w_hbm, gain_hbm,
    dq_ref, dk_ref, dv_ref, wg_ref,
    q_ref, k_ref, v_ref, g_ref, w_ref, gain_ref,
    kx, vx, term, term_in, s_one, s_xy, s_z, s_full,
    w_in, w_rows, w_all, g_in, attn_own, attn_in,
    probs, u_keep, wg_out, wg_in, wg_zout, wg_zin, wg_dp, wg_sum, wg_fin,
    back_out, back_in, dkv_keep,
    lsem, ssem, rsem,
):
    dp = lax.axis_index("dp")
    seq = lax.axis_index("seq")
    core = seq % 2
    z = (seq // 2) % 8
    p = seq // 16
    y = p // 4
    other = 1 - core
    partner = seq + 1 - 2 * core
    after = (seq + 1) % N_SEQ
    before = (seq + N_SEQ - 1) % N_SEQ
    factor = DH ** (-0.5)

    loads = [
        pltpu.make_async_copy(src, dst, lsem.at[i])
        for i, (src, dst) in enumerate(
            (
                (k_hbm, k_ref),
                (v_hbm, v_ref),
                (w_hbm, w_ref),
                (q_hbm, q_ref),
                (gain_hbm, gain_ref),
                (g_hbm, g_ref),
            )
        )
    ]
    for load in loads:
        load.start()

    def xy_peer(d):
        return (((p + d) % 8) * 8 + z) * 2 + core

    def z_peer(d):
        return (p * 8 + (z + d) % 8) * 2 + core

    def z_cross(d):
        return (p * 8 + (z + d) % 8) * 2 + other

    y_peer = xy_peer(4)
    y_cross = (((p + 4) % 8) * 8 + z) * 2 + other

    barrier = pltpu.get_barrier_semaphore()
    peers = [((dp + d) % N_DP, seq) for d in (2, 1, 3)]
    peers += [(dp, z_peer(d)) for d in FAR]
    peers += [(dp, z_cross(d)) for d in FAR]
    peers += [(dp, xy_peer(d)) for d in FAR]
    peers += [(dp, partner), (dp, after), (dp, before), (dp, y_cross)]
    for peer in peers:
        pl.semaphore_signal(barrier, inc=1, device_id=peer, device_id_type=MESH)

    used = [0]
    started = []

    def send(src, dst, device, dp_to=None):
        index = used[0]
        used[0] += 1
        copy = pltpu.make_async_remote_copy(
            src_ref=src,
            dst_ref=dst,
            send_sem=ssem.at[index],
            recv_sem=rsem.at[index],
            device_id=(dp if dp_to is None else dp_to, device),
            device_id_type=MESH,
        )
        copy.start()
        started.append(copy)
        return copy

    def arrived(copies):
        for copy in copies:
            copy.wait_recv()

    class Total:
        def __init__(self, slot, terms):
            self.i = slot
            for h in range(2):
                term[slot, h] = terms[h]

        def start(self):
            i = self.i
            self.c = [send(term.at[i, other], term_in.at[i], partner)]

        def xy(self):
            i = self.i
            arrived(self.c)
            s_one[i] = (term[i, core] + term_in[i]).reshape(8, 16, DH)
            self.c = [send(s_one.at[i, (p + d) % 8], s_xy.at[i, d], xy_peer(d)) for d in FAR]

        def along_z(self):
            i = self.i
            arrived(self.c)
            total = s_one[i, p]
            for d in range(1, 8):
                total = total + s_xy[i, d]
            s_z[i, z] = total
            self.c = [send(s_z.at[i, z], s_z.at[i, z], z_peer(d)) for d in FAR]

        def spread(self):
            i = self.i
            arrived(self.c)
            total = s_z[i, 0]
            for d in range(1, 8):
                total = total + s_z[i, d]
            s_full[i, core, p] = total
            mine = s_full.at[i, core, p]
            self.c = [send(mine, mine, xy_peer(d)) for d in FAR]

        def swap(self):
            i = self.i
            arrived(self.c)
            mine = s_full.at[i, core]
            self.c = [send(mine, mine, partner)]

        def value(self):
            arrived(self.c)
            return [s_full[self.i, h].reshape(DH, DH) for h in range(2)]

    class Half:
        def __init__(self, half, g_mine, g_other):
            self.s = s = half
            for b in range(4):
                rows = slice(s * SOFT + b * 64, s * SOFT + (b + 1) * 64)
                block = dot(attn_own[:, rows], g_mine, 0, 0) + dot(attn_in[:, rows], g_other, 0, 0)
                block = block.astype(BF16)
                wg_out[s, b] = block[:, 0:256]
                wg_out[s, 4 + b] = block[:, 256:512]

        def xy(self):
            s = self.s
            self.c = [send(wg_out.at[s, (p + d) % 8], wg_in.at[s, d], xy_peer(d)) for d in FAR]

        def along_z(self):
            s = self.s
            arrived(self.c)
            total = wg_out[s, p].astype(F32)
            for d in range(1, 8):
                total = total + wg_in[s, d].astype(F32)
            wg_zout[s] = total.reshape(8, 8, 256)
            self.c = [send(wg_zout.at[s, (z + d) % 8], wg_zin.at[s, d], z_peer(d)) for d in FAR]

        def plasmids(self):
            s = self.s
            arrived(self.c)
            total = wg_zout[s, z]
            for d in range(1, 8):
                total = total + wg_zin[s, d]
            wg_dp[s, dp] = total
            mine = wg_dp.at[s, dp]
            self.c = [send(mine, mine, seq, (dp + d) % N_DP) for d in (2, 1, 3)]

        def value(self):
            s = self.s
            arrived(self.c)
            total = (wg_dp[s, 0] + wg_dp[s, 1]) + (wg_dp[s, 2] + wg_dp[s, 3])
            wg_sum[s] = total * (1.0 / math.sqrt(N_DP * N_SEQ * ROWS))

    loads[0].wait()
    loads[1].wait()
    state_sum = Total(
        0,
        [
            dot_wide(unit_plus(k_ref[:, head(2 + h)].astype(F32)), v_ref[:, head(2 + h)], 0, 0)
            for h in range(2)
        ],
    )
    loads[2].wait()
    w_in[z * 2 + core] = jnp.where(
        core == 0, w_ref[:, 0:512].astype(F32), w_ref[:, 512:1024].astype(F32)
    ).astype(BF16)

    pl.semaphore_wait(barrier, len(peers))

    state_sum.start()
    w_mine = w_hbm.at[:, pl.ds(pl.multiple_of(core * 512, 512), 512)]
    w_cross = w_hbm.at[:, pl.ds(pl.multiple_of(other * 512, 512), 512)]
    w_slot = w_in.at[z * 2 + core]
    w_copy = [send(w_cross, w_slot, partner)]
    for d in FAR:
        w_copy.append(send(w_mine, w_slot, z_peer(d)))
        w_copy.append(send(w_cross, w_slot, z_cross(d)))
    soft = pl.ds(0, SOFT)
    k_copy = [
        send(k_hbm.at[:, soft], kx.at[0], after),
        send(k_hbm.at[:, soft], kx.at[1], before),
    ]
    v_copy = [
        send(v_hbm.at[:, soft], vx.at[0], after),
        send(v_hbm.at[:, soft], vx.at[1], before),
    ]
    g_copy = [
        send(g_hbm.at[:, pl.ds(pl.multiple_of(other * 512, 512), 512)], g_in, partner)
    ]
    for load in loads[3:]:
        load.wait()

    state_sum.xy()

    row_pos = lax.broadcasted_iota(jnp.int32, (ROWS, ROWS), 0)
    col_pos = lax.broadcasted_iota(jnp.int32, (ROWS, ROWS), 1)
    keep = (col_pos >= row_pos, None, col_pos < row_pos)
    arrived(k_copy)

    def span_of(halo, ref, h):
        return (halo[0, :, head(h)], ref[:, head(h)], halo[1, :, head(h)])

    for h in range(2):
        k_span = span_of(kx, k_ref, h)
        q_h = q_ref[:, head(h)]
        scores = []
        for b in range(3):
            s = dot(q_h, k_span[b], 1, 1) * factor
            scores.append(s if keep[b] is None else jnp.where(keep[b], s, -1e30))
        peak = jnp.max(jnp.maximum(jnp.maximum(scores[0], scores[1]), scores[2]), axis=1, keepdims=True)
        terms = []
        for b in range(3):
            e = jnp.exp(scores[b] - peak)
            terms.append(e if keep[b] is None else jnp.where(keep[b], e, 0.0))
        whole = jnp.sum(terms[0] + terms[1] + terms[2], axis=1, keepdims=True)
        for b in range(3):
            probs[h, b] = terms[b] / whole

    state_sum.along_z()

    arrived(w_copy)
    for i in range(16):
        w_rows[4 * i : 4 * i + 4, :] = w_in[i].astype(F32)

    def w_block(source):
        return w_all.at[core, pl.ds(pl.multiple_of(source * 64, 64), 64), :]

    w_all[core, pl.ds(pl.multiple_of(p * 64, 64), 64), :] = w_rows[...].astype(BF16)
    w_copy = {d: send(w_block(p), w_block(p), xy_peer(d)) for d in FAR}
    w_swap = [send(w_block(p), w_block(p), partner)]

    arrived(v_copy)
    for h in range(2):
        v_span = span_of(vx, v_ref, h)
        total = dot(probs[h, 0].astype(BF16), v_span[0], 1, 0)
        for b in range(1, 3):
            total = total + dot(probs[h, b].astype(BF16), v_span[b], 1, 0)
        attn_own[:, head(h)] = total.astype(BF16)
    a_copy = [send(attn_own.at[:, soft], attn_in.at[:, soft], partner)]

    state_sum.spread()

    arrived(g_copy)
    arrived(a_copy)
    g_mine = g_ref[:, pl.ds(pl.multiple_of(core * 512, 512), 512)]
    wg_soft = Half(0, g_mine, g_in[...])
    wg_soft.xy()

    for d in FAR[::-1]:
        w_copy[d].wait_recv()
        block = w_block((p + 8 - d) % 8)
        w_swap.append(send(block, block, partner))

    state_sum.swap()
    state = state_sum.value()

    phi_q = []
    lin_r = []
    for h in range(2):
        q_lin = q_ref[:, head(2 + h)].astype(F32)
        phi_q.append(unit_plus(q_lin))
        u = dot_wide(phi_q[h], state[h], 1, 0)
        r = lax.rsqrt(jnp.mean(u * u, axis=1, keepdims=True) + norm_eps)
        u_keep[h] = u
        lin_r.append(r)
        attn_own[:, head(2 + h)] = (gain_ref[h : h + 1, :] * u * r).astype(BF16)
    lin = pl.ds(SOFT, SOFT)
    a_copy = [send(attn_own.at[:, lin], attn_in.at[:, lin], partner)]

    arrived(w_swap)
    d_attn = (dot(g_ref[:, 0:512], w_all[0], 1, 1) + dot(g_ref[:, 512:1024], w_all[1], 1, 1)).astype(BF16)

    grad_u = []
    for h in range(2):
        g_lin = gain_ref[h : h + 1, :] * d_attn[:, head(2 + h)].astype(F32)
        u = u_keep[h]
        r = lin_r[h]
        grad_u.append(r * g_lin - u * (r * r * r) * jnp.mean(g_lin * u, axis=1, keepdims=True))
    grad_sum = Total(1, [dot_wide(phi_q[h], grad_u[h], 0, 0) for h in range(2)])
    grad_sum.start()

    arrived(a_copy)
    wg_lin = Half(1, g_mine, g_in[...])
    grad_sum.xy()
    wg_lin.xy()
    wg_soft.along_z()

    for h in range(2):
        k_span = span_of(kx, k_ref, h)
        v_span = span_of(vx, v_ref, h)
        q_h = q_ref[:, head(h)]
        da = d_attn[:, head(h)]
        delta = jnp.sum(da.astype(F32) * attn_own[:, head(h)].astype(F32), axis=1, keepdims=True)
        dq = None
        for b in range(3):
            pr = probs[h, b]
            ds = (pr * (dot(da, v_span[b], 1, 1) - delta)).astype(BF16)
            step = dot(ds, k_span[b], 1, 0)
            dq = step if dq is None else dq + step
            dk = dot(ds, q_h, 0, 0) * factor
            dv = dot(pr.astype(BF16), da, 0, 0)
            if b == 1:
                dkv_keep[0, :, head(h)] = dk
                dkv_keep[1, :, head(h)] = dv
            else:
                back_out[b // 2, 0, :, head(h)] = dk.astype(BF16)
                back_out[b // 2, 1, :, head(h)] = dv.astype(BF16)
        dq_ref[:, head(h)] = (dq * factor).astype(BF16)
    back_copy = [
        send(back_out.at[0], back_in.at[0], before),
        send(back_out.at[1], back_in.at[1], after),
    ]

    grad_sum.along_z()

    for h in range(2):
        q_lin = q_ref[:, head(2 + h)].astype(F32)
        dq_lin = dot_wide(grad_u[h], state[h], 1, 1) * unit_slope(q_lin)
        dq_ref[:, head(2 + h)] = dq_lin.astype(BF16)

    wg_lin.along_z()
    wg_soft.plasmids()
    grad_sum.spread()

    arrived(back_copy)
    for h in range(2):
        for t, out in ((0, dk_ref), (1, dv_ref)):
            total = dkv_keep[t, :, head(h)] + back_in[1, t, :, head(h)].astype(F32)
            total = total + back_in[0, t, :, head(h)].astype(F32)
            out[:, head(h)] = total.astype(BF16)

    wg_lin.plasmids()
    grad_sum.swap()
    dstate = grad_sum.value()
    for h in range(2):
        k_l = k_ref[:, head(2 + h)].astype(F32)
        v_l = v_ref[:, head(2 + h)]
        dk_lin = dot_wide(v_l, dstate[h], 1, 1) * unit_slope(k_l)
        dk_ref[:, head(2 + h)] = dk_lin.astype(BF16)
        dv_ref[:, head(2 + h)] = dot_wide(unit_plus(k_l), dstate[h], 1, 0).astype(BF16)

    wg_soft.value()
    wg_lin.value()
    wg_fin[core, y] = wg_sum[y]
    slot = wg_fin.at[core, y]
    fin_copy = [
        send(wg_sum.at[1 - y], slot, y_peer),
        send(wg_sum.at[1 - y], slot, y_cross),
        send(wg_sum.at[y], slot, partner),
    ]
    arrived(fin_copy)
    for c in range(2):
        for half in range(2):
            rows = wg_fin[c, half]
            first = c * 512 + half * 256
            wg_ref[:, first : first + 256] = jnp.where(core == 0, rows[0:4], rows[4:8])
    for copy in started:
        copy.wait_send()
    assert used[0] == N_COPIES, used[0]


N_COPIES = (
    2 * (1 + 7 + 7 + 7 + 1)
    + 15 + 7 + 8
    + 4 + 1 + 2
    + 2 * (7 + 7 + 3) + 3
    + 2
)


def writer(dq, dk, dv, wg, dq_out, dk_out, dv_out, wg_out, sem):
    copies = [
        pltpu.make_async_copy(src, dst, sem.at[i])
        for i, (src, dst) in enumerate(((dq, dq_out), (dk, dk_out), (dv, dv_out), (wg, wg_out)))
    ]
    for copy in copies:
        copy.start()
    for copy in copies:
        copy.wait()


RESULTS = (((ROWS, 512), BF16), ((ROWS, 512), BF16), ((ROWS, 512), BF16), ((4, 1024), F32))


def body(queries, key_rows, value_rows, out_grad, out_weight, norm_gain):
    vmem = pl.BlockSpec(memory_space=pltpu.VMEM)
    hbm = pl.BlockSpec(memory_space=pltpu.HBM)
    out = pl.pallas_call(
        kernel,
        out_shape=tuple(pltpu.VMEM(*result) for result in RESULTS),
        in_specs=[hbm] * 6,
        out_specs=(vmem,) * 4,
        scratch_shapes=[
            pltpu.VMEM((ROWS, 512), BF16),
            pltpu.VMEM((ROWS, 512), BF16),
            pltpu.VMEM((ROWS, 512), BF16),
            pltpu.VMEM((ROWS, 1024), BF16),
            pltpu.VMEM((4, 1024), BF16),
            pltpu.VMEM((2, DH), F32),
            pltpu.VMEM((2, ROWS, SOFT), BF16),
            pltpu.VMEM((2, ROWS, SOFT), BF16),
            pltpu.VMEM((2, 2, DH, DH), F32),
            pltpu.VMEM((2, DH, DH), F32),
            pltpu.VMEM((2, 8, 16, DH), F32),
            pltpu.VMEM((2, 8, 16, DH), F32),
            pltpu.VMEM((2, 8, 16, DH), F32),
            pltpu.VMEM((2, 2, 8, 16, DH), F32),
            pltpu.VMEM((16, 4, 512), BF16),
            pltpu.VMEM((64, 512), F32),
            pltpu.VMEM((2, 512, 512), BF16),
            pltpu.VMEM((ROWS, 512), BF16),
            pltpu.VMEM((ROWS, 512), BF16),
            pltpu.VMEM((ROWS, 512), BF16),
            pltpu.VMEM((2, 3, ROWS, ROWS), F32),
            pltpu.VMEM((2, ROWS, DH), F32),
            pltpu.VMEM((2, 8, 64, 256), BF16),
            pltpu.VMEM((2, 8, 64, 256), BF16),
            pltpu.VMEM((2, 8, 8, 256), F32),
            pltpu.VMEM((2, 8, 8, 256), F32),
            pltpu.VMEM((2, N_DP, 8, 256), F32),
            pltpu.VMEM((2, 8, 256), F32),
            pltpu.VMEM((2, 2, 8, 256), F32),
            pltpu.VMEM((2, 2, ROWS, SOFT), BF16),
            pltpu.VMEM((2, 2, ROWS, SOFT), BF16),
            pltpu.VMEM((2, ROWS, SOFT), F32),
            pltpu.SemaphoreType.DMA((6,)),
            pltpu.SemaphoreType.DMA((N_COPIES,)),
            pltpu.SemaphoreType.DMA((N_COPIES,)),
        ],
        compiler_params=pltpu.CompilerParams(collective_id=0, has_side_effects=True),
        name="sublayer_backward",
    )(
        queries[0],
        key_rows[0],
        value_rows[0],
        out_grad[0],
        out_weight,
        norm_gain.reshape(2, DH),
    )
    out = pl.pallas_call(
        writer,
        out_shape=tuple(jax.ShapeDtypeStruct(*result) for result in RESULTS),
        in_specs=[vmem] * 4,
        out_specs=(hbm,) * 4,
        scratch_shapes=[pltpu.SemaphoreType.DMA((4,))],
        name="write_out",
    )(*[pltpu.with_memory_space_constraint(x, pltpu.VMEM) for x in out])
    return (out[0][None], out[1][None], out[2][None], out[3])


def solution(mesh):
    return jax.shard_map(
        body,
        mesh=mesh,
        in_specs=(
            P("dp", "seq", None),
            P("dp", "seq", None),
            P("dp", "seq", None),
            P("dp", "seq", None),
            P("seq", None),
            P(),
        ),
        out_specs=(
            P("dp", "seq", None),
            P("dp", "seq", None),
            P("dp", "seq", None),
            P("seq", None),
        ),
        check_vma=False,
    )
```

profile of v0, /device:TPU:1, one launch (start us, length us, event | category | flops | bytes accessed | tf_op | source)
XLA Modules:
  0.0 56.6 jit_solution(12460636420279674407)
XLA Ops:
  0.6 55.2 %sublayer_backward.1 = (bf16[128,512]{1,0:T(8,128)(2,1)S(1)}, bf16[128,512]{1,0:T(8,128)(2,1)S(1)}, bf16[128,512]{1,0:T(8,128)(2,1)S(1)}, f32[4,1024]{1,0:T(4,128)S(1)}) custom-call(bf16[128,512]{1,0:T(8,128)(2,1)} %bitcast.9, bf16[128,512]{1,0:T(8,128)(2,1)} %bitcast.10, bf16[128,512]{1,0:T(8,128)(2,1)} %bitcast.11, bf16[128,1024]{1,0:T(8,128)(2,1)} %bitcast.8, ...), custom_call_target="tpu_custom_call" | custom-call | tf_op jit(solution)/shard_map/sublayer_backward/pallas_call | solution.py:458
  55.8 0.8 %write_out.1 = (bf16[128,512]{1,0:T(8,128)(2,1)}, bf16[128,512]{1,0:T(8,128)(2,1)}, bf16[128,512]{1,0:T(8,128)(2,1)}, f32[4,1024]{1,0:T(4,128)}) custom-call(bf16[128,512]{1,0:T(8,128)(2,1)S(1)} %get-tuple-element.12.dq, bf16[128,512]{1,0:T(8,128)(2,1)S(1)} %get-tuple-element.13.dk, bf16[128,512]{1,0:T(8,128)(2,1)S(1)} %get-tuple-element.14.dv, ...), custom_call_target="tpu_custom_call" | custom-call | tf_op jit(solution)/shard_map/write_out/pallas_call | solution.py:510
where the time goes:
time: 56.7 us; the launch traced here: 56.6 us
  Pallas kernels  55.9 us (99%)
  between operations  0.64 us (1%)
    pallas_call x1, Pallas kernels, body(): pl.pallas_call(kernel, out_shape=tuple((pltpu.VMEM(*result) for result in...  55.2 us

commit v1 on v0

--- a/solution.py
+++ b/solution.py
@@ -62,7 +62,7 @@
     q_ref, k_ref, v_ref, g_ref, w_ref, gain_ref,
     kx, vx, term, term_in, s_one, s_xy, s_z, s_full,
     w_in, w_rows, w_all, g_in, attn_own, attn_in,
-    probs, u_keep, wg_out, wg_in, wg_zout, wg_zin, wg_dp, wg_sum, wg_fin,
+    probs, u_keep, wg_out, wg_in, wg_zout, wg_zin, wg_sum, wg_fin,
     back_out, back_in, dkv_keep,
     lsem, ssem, rsem,
 ):
@@ -103,20 +103,26 @@
     def z_cross(d):
         return (p * 8 + (z + d) % 8) * 2 + other
 
-    y_peer = xy_peer(4)
-    y_cross = (((p + 4) % 8) * 8 + z) * 2 + other
+    def column_peer(step):
+        to_dp, flip, cross = step
+        chip = ((p + 4 * flip) % 8) * 8 + z
+        return (dp + to_dp) % N_DP, chip * 2 + (core + cross) % 2
+
+    steps = [(a, b, c) for a in (2, 1, 3, 0) for b in range(2) for c in range(2)][:-4]
+    steps += [(0, 1, 1), (0, 1, 0), (0, 0, 1)]
 
     barrier = pltpu.get_barrier_semaphore()
-    peers = [((dp + d) % N_DP, seq) for d in (2, 1, 3)]
+    peers = [column_peer(step) for step in steps]
     peers += [(dp, z_peer(d)) for d in FAR]
     peers += [(dp, z_cross(d)) for d in FAR]
     peers += [(dp, xy_peer(d)) for d in FAR]
-    peers += [(dp, partner), (dp, after), (dp, before), (dp, y_cross)]
+    peers += [(dp, after), (dp, before)]
     for peer in peers:
         pl.semaphore_signal(barrier, inc=1, device_id=peer, device_id_type=MESH)
 
     used = [0]
     started = []
+    fin_base = N_COPIES
 
     def send(src, dst, device, dp_to=None):
         index = used[0]
@@ -205,21 +211,49 @@
             wg_zout[s] = total.reshape(8, 8, 256)
             self.c = [send(wg_zout.at[s, (z + d) % 8], wg_zin.at[s, d], z_peer(d)) for d in FAR]
 
-        def plasmids(self):
+        def deliver(self):
             s = self.s
             arrived(self.c)
             total = wg_zout[s, z]
             for d in range(1, 8):
                 total = total + wg_zin[s, d]
-            wg_dp[s, dp] = total
-            mine = wg_dp.at[s, dp]
-            self.c = [send(mine, mine, seq, (dp + d) % N_DP) for d in (2, 1, 3)]
-
-        def value(self):
-            s = self.s
-            arrived(self.c)
-            total = (wg_dp[s, 0] + wg_dp[s, 1]) + (wg_dp[s, 2] + wg_dp[s, 3])
-            wg_sum[s] = total * (1.0 / math.sqrt(N_DP * N_SEQ * ROWS))
+            for c in range(2):
+                wg_sum[s, c] = total[4 * c : 4 * c + 4]
+            flip = (s + y) % 2
+            owner = ((s * 4 + p % 4) * 8 + z) * 2
+
+            def copy_to(to_dp, cross):
+                index = fin_base + flip * 8 + to_dp * 2 + cross
+                core_to = (core + cross) % 2
+                return pltpu.make_async_remote_copy(
+                    src_ref=wg_sum.at[s, core_to],
+                    dst_ref=wg_fin.at[dp, core, y],
+                    send_sem=ssem.at[index],
+                    recv_sem=rsem.at[index],
+                    device_id=((dp + to_dp) % N_DP, owner + core_to),
+                    device_id_type=MESH,
+                )
+
+            self.out = [copy_to(a, c) for a in (2, 1, 3) for c in range(2)] + [copy_to(0, 1)]
+            for copy in self.out:
+                copy.start()
+            self.last = copy_to(0, 0)
+
+            @pl.when(flip == 1)
+            def _():
+                self.last.start()
+
+            @pl.when(flip == 0)
+            def _():
+                wg_fin[dp, core, y] = wg_sum[s, core]
+
+        def finish(self):
+            for copy in self.out:
+                copy.wait_send()
+
+            @pl.when((self.s + y) % 2 == 1)
+            def _():
+                self.last.wait_send()
 
     loads[0].wait()
     loads[1].wait()
@@ -337,22 +371,27 @@
     lin = pl.ds(SOFT, SOFT)
     a_copy = [send(attn_own.at[:, lin], attn_in.at[:, lin], partner)]
 
+    mine_lin = dot(g_mine, w_all[core, SOFT:512, :], 1, 1)
+    arrived(a_copy)
+    wg_lin = Half(1, g_mine, g_in[...])
+    wg_lin.xy()
+
     arrived(w_swap)
-    d_attn = (dot(g_ref[:, 0:512], w_all[0], 1, 1) + dot(g_ref[:, 512:1024], w_all[1], 1, 1)).astype(BF16)
+    g_cross = g_ref[:, pl.ds(pl.multiple_of(other * 512, 512), 512)]
+    d_attn_lin = (mine_lin + dot(g_cross, w_all[other, SOFT:512, :], 1, 1)).astype(BF16)
 
     grad_u = []
     for h in range(2):
-        g_lin = gain_ref[h : h + 1, :] * d_attn[:, head(2 + h)].astype(F32)
+        g_lin = gain_ref[h : h + 1, :] * d_attn_lin[:, head(h)].astype(F32)
         u = u_keep[h]
         r = lin_r[h]
         grad_u.append(r * g_lin - u * (r * r * r) * jnp.mean(g_lin * u, axis=1, keepdims=True))
     grad_sum = Total(1, [dot_wide(phi_q[h], grad_u[h], 0, 0) for h in range(2)])
     grad_sum.start()
 
-    arrived(a_copy)
-    wg_lin = Half(1, g_mine, g_in[...])
+    d_attn = dot(g_ref[:, 0:512], w_all[0, 0:SOFT, :], 1, 1) + dot(g_ref[:, 512:1024], w_all[1, 0:SOFT, :], 1, 1)
+    d_attn = d_attn.astype(BF16)
     grad_sum.xy()
-    wg_lin.xy()
     wg_soft.along_z()
 
     for h in range(2):
@@ -389,7 +428,7 @@
         dq_ref[:, head(2 + h)] = dq_lin.astype(BF16)
 
     wg_lin.along_z()
-    wg_soft.plasmids()
+    wg_soft.deliver()
     grad_sum.spread()
 
     arrived(back_copy)
@@ -399,7 +438,7 @@
             total = total + back_in[0, t, :, head(h)].astype(F32)
             out[:, head(h)] = total.astype(BF16)
 
-    wg_lin.plasmids()
+    wg_lin.deliver()
     grad_sum.swap()
     dstate = grad_sum.value()
     for h in range(2):
@@ -409,21 +448,24 @@
         dk_ref[:, head(2 + h)] = dk_lin.astype(BF16)
         dv_ref[:, head(2 + h)] = dot_wide(unit_plus(k_l), dstate[h], 1, 0).astype(BF16)
 
-    wg_soft.value()
-    wg_lin.value()
-    wg_fin[core, y] = wg_sum[y]
-    slot = wg_fin.at[core, y]
-    fin_copy = [
-        send(wg_sum.at[1 - y], slot, y_peer),
-        send(wg_sum.at[1 - y], slot, y_cross),
-        send(wg_sum.at[y], slot, partner),
-    ]
-    arrived(fin_copy)
+    for step in steps:
+        to_dp, flip, cross = step
+        index = fin_base + flip * 8 + to_dp * 2 + cross
+        pltpu.make_async_remote_copy(
+            src_ref=wg_sum.at[0, 0],
+            dst_ref=wg_fin.at[0, 0, 0],
+            send_sem=ssem.at[index],
+            recv_sem=rsem.at[index],
+            device_id=column_peer(step),
+            device_id_type=MESH,
+        ).wait_recv()
     for c in range(2):
         for half in range(2):
-            rows = wg_fin[c, half]
+            total = (wg_fin[0, c, half] + wg_fin[1, c, half]) + (wg_fin[2, c, half] + wg_fin[3, c, half])
             first = c * 512 + half * 256
-            wg_ref[:, first : first + 256] = jnp.where(core == 0, rows[0:4], rows[4:8])
+            wg_ref[:, first : first + 256] = total * (1.0 / math.sqrt(N_DP * N_SEQ * ROWS))
+    wg_soft.finish()
+    wg_lin.finish()
     for copy in started:
         copy.wait_send()
     assert used[0] == N_COPIES, used[0]
@@ -433,7 +475,7 @@
     2 * (1 + 7 + 7 + 7 + 1)
     + 15 + 7 + 8
     + 4 + 1 + 2
-    + 2 * (7 + 7 + 3) + 3
+    + 2 * (7 + 7)
     + 2
 )
 
@@ -487,15 +529,14 @@
             pltpu.VMEM((2, 8, 64, 256), BF16),
             pltpu.VMEM((2, 8, 8, 256), F32),
             pltpu.VMEM((2, 8, 8, 256), F32),
-            pltpu.VMEM((2, N_DP, 8, 256), F32),
-            pltpu.VMEM((2, 8, 256), F32),
-            pltpu.VMEM((2, 2, 8, 256), F32),
+            pltpu.VMEM((2, 2, 4, 256), F32),
+            pltpu.VMEM((N_DP, 2, 2, 4, 256), F32),
             pltpu.VMEM((2, 2, ROWS, SOFT), BF16),
             pltpu.VMEM((2, 2, ROWS, SOFT), BF16),
             pltpu.VMEM((2, ROWS, SOFT), F32),
             pltpu.SemaphoreType.DMA((6,)),
-            pltpu.SemaphoreType.DMA((N_COPIES,)),
-            pltpu.SemaphoreType.DMA((N_COPIES,)),
+            pltpu.SemaphoreType.DMA((N_COPIES + 16,)),
+            pltpu.SemaphoreType.DMA((N_COPIES + 16,)),
         ],
         compiler_params=pltpu.CompilerParams(collective_id=0, has_side_effects=True),
         name="sublayer_backward",

time: 56.7 us -> 55 us (0.970)
  Pallas kernels: 55.9 us -> 54.2 us
    pallas_call x1, Pallas kernels: 55.2 us -> 53.4 us  [body(): pl.pallas_call(kernel, out_shape=tuple((pltpu.VMEM(*result) for result in...]
where the time goes in v1:
time: 55 us; the launch traced here: 54.8 us
  Pallas kernels  54.2 us (99%)
  between operations  0.64 us (1%)
    pallas_call x1, Pallas kernels, body(): pl.pallas_call(kernel, out_shape=tuple((pltpu.VMEM(*result) for result in...  53.4 us

profile of v1, /device:TPU:1, one launch (start us, length us, event | category | flops | bytes accessed | tf_op | source)
XLA Modules:
  0.0 54.8 jit_solution(4621441516224506716)
XLA Ops:
  0.6 53.4 %sublayer_backward.1 = (bf16[128,512]{1,0:T(8,128)(2,1)S(1)}, bf16[128,512]{1,0:T(8,128)(2,1)S(1)}, bf16[128,512]{1,0:T(8,128)(2,1)S(1)}, f32[4,1024]{1,0:T(4,128)S(1)}) custom-call(bf16[128,512]{1,0:T(8,128)(2,1)} %bitcast.9, bf16[128,512]{1,0:T(8,128)(2,1)} %bitcast.10, bf16[128,512]{1,0:T(8,128)(2,1)} %bitcast.11, bf16[128,1024]{1,0:T(8,128)(2,1)} %bitcast.8, ...), custom_call_target="tpu_custom_call" | custom-call | tf_op jit(solution)/shard_map/sublayer_backward/pallas_call | solution.py:500
  54.1 0.8 %write_out.1 = (bf16[128,512]{1,0:T(8,128)(2,1)}, bf16[128,512]{1,0:T(8,128)(2,1)}, bf16[128,512]{1,0:T(8,128)(2,1)}, f32[4,1024]{1,0:T(4,128)}) custom-call(bf16[128,512]{1,0:T(8,128)(2,1)S(1)} %get-tuple-element.12.dq, bf16[128,512]{1,0:T(8,128)(2,1)S(1)} %get-tuple-element.13.dk, bf16[128,512]{1,0:T(8,128)(2,1)S(1)} %get-tuple-element.14.dv, ...), custom_call_target="tpu_custom_call" | custom-call | tf_op jit(solution)/shard_map/write_out/pallas_call | solution.py:551

commit v2 on v1

--- a/solution.py
+++ b/solution.py
@@ -60,7 +60,7 @@
     q_hbm, k_hbm, v_hbm, g_hbm, w_hbm, gain_hbm,
     dq_ref, dk_ref, dv_ref, wg_ref,
     q_ref, k_ref, v_ref, g_ref, w_ref, gain_ref,
-    kx, vx, term, term_in, s_one, s_xy, s_z, s_full,
+    kx, vx, phi_part, phi_turned, term, s_xy, s_z, s_full,
     w_in, w_rows, w_all, g_in, attn_own, attn_in,
     probs, u_keep, wg_out, wg_in, wg_zout, wg_zin, wg_sum, wg_fin,
     back_out, back_in, dkv_keep,
@@ -97,6 +97,9 @@
     def xy_peer(d):
         return (((p + d) % 8) * 8 + z) * 2 + core
 
+    def flat_peer(d, cross):
+        return (((p + d) % 8) * 8 + z) * 2 + (core + cross) % 2
+
     def z_peer(d):
         return (p * 8 + (z + d) % 8) * 2 + core
 
@@ -115,7 +118,7 @@
     peers = [column_peer(step) for step in steps]
     peers += [(dp, z_peer(d)) for d in FAR]
     peers += [(dp, z_cross(d)) for d in FAR]
-    peers += [(dp, xy_peer(d)) for d in FAR]
+    peers += [(dp, flat_peer(d, cross)) for d in FAR if d != 4 for cross in range(2)]
     peers += [(dp, after), (dp, before)]
     for peer in peers:
         pl.semaphore_signal(barrier, inc=1, device_id=peer, device_id_type=MESH)
@@ -143,46 +146,39 @@
         for copy in copies:
             copy.wait_recv()
 
+    near = [(d, cross) for d in FAR for cross in range(2)] + [(0, 1)]
+
     class Total:
         def __init__(self, slot, terms):
             self.i = slot
             for h in range(2):
-                term[slot, h] = terms[h]
+                term[slot, h] = terms[h].astype(BF16).reshape(8, 16, DH)
 
         def start(self):
             i = self.i
-            self.c = [send(term.at[i, other], term_in.at[i], partner)]
-
-        def xy(self):
-            i = self.i
-            arrived(self.c)
-            s_one[i] = (term[i, core] + term_in[i]).reshape(8, 16, DH)
-            self.c = [send(s_one.at[i, (p + d) % 8], s_xy.at[i, d], xy_peer(d)) for d in FAR]
+            self.c = [
+                send(term.at[i, (core + cross) % 2, (p + d) % 8], s_xy.at[i, d, cross], flat_peer(d, cross))
+                for d, cross in near
+            ]
 
         def along_z(self):
             i = self.i
             arrived(self.c)
-            total = s_one[i, p]
-            for d in range(1, 8):
-                total = total + s_xy[i, d]
-            s_z[i, z] = total
+            total = term[i, core, p].astype(F32)
+            for d, cross in near[::-1]:
+                total = total + s_xy[i, d, cross].astype(F32)
+            s_z[i, z] = total.astype(BF16)
             self.c = [send(s_z.at[i, z], s_z.at[i, z], z_peer(d)) for d in FAR]
 
         def spread(self):
             i = self.i
             arrived(self.c)
-            total = s_z[i, 0]
+            total = s_z[i, 0].astype(F32)
             for d in range(1, 8):
-                total = total + s_z[i, d]
-            s_full[i, core, p] = total
+                total = total + s_z[i, d].astype(F32)
+            s_full[i, core, p] = total.astype(BF16)
             mine = s_full.at[i, core, p]
-            self.c = [send(mine, mine, xy_peer(d)) for d in FAR]
-
-        def swap(self):
-            i = self.i
-            arrived(self.c)
-            mine = s_full.at[i, core]
-            self.c = [send(mine, mine, partner)]
+            self.c = [send(mine, mine, flat_peer(d, cross)) for d, cross in near]
 
         def value(self):
             arrived(self.c)
@@ -208,15 +204,15 @@
             total = wg_out[s, p].astype(F32)
             for d in range(1, 8):
                 total = total + wg_in[s, d].astype(F32)
-            wg_zout[s] = total.reshape(8, 8, 256)
+            wg_zout[s] = total.reshape(8, 8, 256).astype(BF16)
             self.c = [send(wg_zout.at[s, (z + d) % 8], wg_zin.at[s, d], z_peer(d)) for d in FAR]
 
         def deliver(self):
             s = self.s
             arrived(self.c)
-            total = wg_zout[s, z]
+            total = wg_zout[s, z].astype(F32)
             for d in range(1, 8):
-                total = total + wg_zin[s, d]
+                total = total + wg_zin[s, d].astype(F32)
             for c in range(2):
                 wg_sum[s, c] = total[4 * c : 4 * c + 4]
             flip = (s + y) % 2
@@ -294,7 +290,23 @@
     for load in loads[3:]:
         load.wait()
 
-    state_sum.xy()
+    for h in range(2):
+        for i, part in enumerate(parts(unit_plus(q_ref[:, head(2 + h)].astype(F32)))):
+            phi_part[h, i] = part
+            phi_turned[h, i] = part.T
+
+    state_sum.along_z()
+
+    arrived(w_copy)
+    for i in range(16):
+        w_rows[4 * i : 4 * i + 4, :] = w_in[i].astype(F32)
+
+    def w_block(source):
+        return w_all.at[core, pl.ds(pl.multiple_of(source * 64, 64), 64), :]
+
+    w_all[core, pl.ds(pl.multiple_of(p * 64, 64), 64), :] = w_rows[...].astype(BF16)
+    w_copy = {d: send(w_block(p), w_block(p), xy_peer(d)) for d in FAR}
+    w_swap = [send(w_block(p), w_block(p), partner)]
 
     row_pos = lax.broadcasted_iota(jnp.int32, (ROWS, ROWS), 0)
     col_pos = lax.broadcasted_iota(jnp.int32, (ROWS, ROWS), 1)
@@ -320,19 +332,6 @@
         for b in range(3):
             probs[h, b] = terms[b] / whole
 
-    state_sum.along_z()
-
-    arrived(w_copy)
-    for i in range(16):
-        w_rows[4 * i : 4 * i + 4, :] = w_in[i].astype(F32)
-
-    def w_block(source):
-        return w_all.at[core, pl.ds(pl.multiple_of(source * 64, 64), 64), :]
-
-    w_all[core, pl.ds(pl.multiple_of(p * 64, 64), 64), :] = w_rows[...].astype(BF16)
-    w_copy = {d: send(w_block(p), w_block(p), xy_peer(d)) for d in FAR}
-    w_swap = [send(w_block(p), w_block(p), partner)]
-
     arrived(v_copy)
     for h in range(2):
         v_span = span_of(vx, v_ref, h)
@@ -355,15 +354,11 @@
         block = w_block((p + 8 - d) % 8)
         w_swap.append(send(block, block, partner))
 
-    state_sum.swap()
     state = state_sum.value()
 
-    phi_q = []
     lin_r = []
     for h in range(2):
-        q_lin = q_ref[:, head(2 + h)].astype(F32)
-        phi_q.append(unit_plus(q_lin))
-        u = dot_wide(phi_q[h], state[h], 1, 0)
+        u = dot(phi_part[h, 0], state[h], 1, 0) + dot(phi_part[h, 1], state[h], 1, 0)
         r = lax.rsqrt(jnp.mean(u * u, axis=1, keepdims=True) + norm_eps)
         u_keep[h] = u
         lin_r.append(r)
@@ -372,10 +367,6 @@
     a_copy = [send(attn_own.at[:, lin], attn_in.at[:, lin], partner)]
 
     mine_lin = dot(g_mine, w_all[core, SOFT:512, :], 1, 1)
-    arrived(a_copy)
-    wg_lin = Half(1, g_mine, g_in[...])
-    wg_lin.xy()
-
     arrived(w_swap)
     g_cross = g_ref[:, pl.ds(pl.multiple_of(other * 512, 512), 512)]
     d_attn_lin = (mine_lin + dot(g_cross, w_all[other, SOFT:512, :], 1, 1)).astype(BF16)
@@ -386,12 +377,20 @@
         u = u_keep[h]
         r = lin_r[h]
         grad_u.append(r * g_lin - u * (r * r * r) * jnp.mean(g_lin * u, axis=1, keepdims=True))
-    grad_sum = Total(1, [dot_wide(phi_q[h], grad_u[h], 0, 0) for h in range(2)])
+    terms = []
+    for h in range(2):
+        high, low = parts(grad_u[h])
+        terms.append(
+            dot(phi_turned[h, 0], high, 1, 0) + dot(phi_turned[h, 0], low, 1, 0) + dot(phi_turned[h, 1], high, 1, 0)
+        )
+    grad_sum = Total(1, terms)
     grad_sum.start()
 
+    arrived(a_copy)
+    wg_lin = Half(1, g_mine, g_in[...])
+    wg_lin.xy()
     d_attn = dot(g_ref[:, 0:512], w_all[0, 0:SOFT, :], 1, 1) + dot(g_ref[:, 512:1024], w_all[1, 0:SOFT, :], 1, 1)
     d_attn = d_attn.astype(BF16)
-    grad_sum.xy()
     wg_soft.along_z()
 
     for h in range(2):
@@ -415,13 +414,13 @@
                 back_out[b // 2, 0, :, head(h)] = dk.astype(BF16)
                 back_out[b // 2, 1, :, head(h)] = dv.astype(BF16)
         dq_ref[:, head(h)] = (dq * factor).astype(BF16)
+    grad_sum.along_z()
+
     back_copy = [
         send(back_out.at[0], back_in.at[0], before),
         send(back_out.at[1], back_in.at[1], after),
     ]
 
-    grad_sum.along_z()
-
     for h in range(2):
         q_lin = q_ref[:, head(2 + h)].astype(F32)
         dq_lin = dot_wide(grad_u[h], state[h], 1, 1) * unit_slope(q_lin)
@@ -439,12 +438,11 @@
             out[:, head(h)] = total.astype(BF16)
 
     wg_lin.deliver()
-    grad_sum.swap()
     dstate = grad_sum.value()
     for h in range(2):
         k_l = k_ref[:, head(2 + h)].astype(F32)
         v_l = v_ref[:, head(2 + h)]
-        dk_lin = dot_wide(v_l, dstate[h], 1, 1) * unit_slope(k_l)
+        dk_lin = dot(v_l, dstate[h], 1, 1) * unit_slope(k_l)
         dk_ref[:, head(2 + h)] = dk_lin.astype(BF16)
         dv_ref[:, head(2 + h)] = dot_wide(unit_plus(k_l), dstate[h], 1, 0).astype(BF16)
 
@@ -472,7 +470,7 @@
 
 
 N_COPIES = (
-    2 * (1 + 7 + 7 + 7 + 1)
+    2 * (15 + 7 + 15)
     + 15 + 7 + 8
     + 4 + 1 + 2
     + 2 * (7 + 7)
@@ -511,12 +509,12 @@
             pltpu.VMEM((2, DH), F32),
             pltpu.VMEM((2, ROWS, SOFT), BF16),
             pltpu.VMEM((2, ROWS, SOFT), BF16),
-            pltpu.VMEM((2, 2, DH, DH), F32),
-            pltpu.VMEM((2, DH, DH), F32),
-            pltpu.VMEM((2, 8, 16, DH), F32),
-            pltpu.VMEM((2, 8, 16, DH), F32),
-            pltpu.VMEM((2, 8, 16, DH), F32),
-            pltpu.VMEM((2, 2, 8, 16, DH), F32),
+            pltpu.VMEM((2, 2, ROWS, DH), BF16),
+            pltpu.VMEM((2, 2, DH, ROWS), BF16),
+            pltpu.VMEM((2, 2, 8, 16, DH), BF16),
+            pltpu.VMEM((2, 8, 2, 16, DH), BF16),
+            pltpu.VMEM((2, 8, 16, DH), BF16),
+            pltpu.VMEM((2, 2, 8, 16, DH), BF16),
             pltpu.VMEM((16, 4, 512), BF16),
             pltpu.VMEM((64, 512), F32),
             pltpu.VMEM((2, 512, 512), BF16),
@@ -527,8 +525,8 @@
             pltpu.VMEM((2, ROWS, DH), F32),
             pltpu.VMEM((2, 8, 64, 256), BF16),
             pltpu.VMEM((2, 8, 64, 256), BF16),
-            pltpu.VMEM((2, 8, 8, 256), F32),
-            pltpu.VMEM((2, 8, 8, 256), F32),
+            pltpu.VMEM((2, 8, 8, 256), BF16),
+            pltpu.VMEM((2, 8, 8, 256), BF16),
             pltpu.VMEM((2, 2, 4, 256), F32),
             pltpu.VMEM((N_DP, 2, 2, 4, 256), F32),
             pltpu.VMEM((2, 2, ROWS, SOFT), BF16),

time: 55 us -> 51.8 us (0.942)
  the two profiles are of different devices: /device:TPU:1 before, /device:TPU:9 now
where the time goes in v2:
time: 51.8 us; the launch traced here: 51.6 us
  Pallas kernels  51 us (98%)
  between operations  0.64 us (1%)
    pallas_call x1, Pallas kernels, body(): pl.pallas_call(kernel, out_shape=tuple((pltpu.VMEM(*result) for result in...  50.2 us

profile of v2, /device:TPU:9, one launch (start us, length us, event | category | flops | bytes accessed | tf_op | source)
XLA Modules:
  0.0 51.6 jit_solution(15897729762977980527)
XLA Ops:
  0.6 50.2 %sublayer_backward.1 = (bf16[128,512]{1,0:T(8,128)(2,1)S(1)}, bf16[128,512]{1,0:T(8,128)(2,1)S(1)}, bf16[128,512]{1,0:T(8,128)(2,1)S(1)}, f32[4,1024]{1,0:T(4,128)S(1)}) custom-call(bf16[128,512]{1,0:T(8,128)(2,1)} %bitcast.9, bf16[128,512]{1,0:T(8,128)(2,1)} %bitcast.10, bf16[128,512]{1,0:T(8,128)(2,1)} %bitcast.11, bf16[128,1024]{1,0:T(8,128)(2,1)} %bitcast.8, ...), custom_call_target="tpu_custom_call" | custom-call | tf_op jit(solution)/shard_map/sublayer_backward/pallas_call | solution.py:498
  50.9 0.8 %write_out.1 = (bf16[128,512]{1,0:T(8,128)(2,1)}, bf16[128,512]{1,0:T(8,128)(2,1)}, bf16[128,512]{1,0:T(8,128)(2,1)}, f32[4,1024]{1,0:T(4,128)}) custom-call(bf16[128,512]{1,0:T(8,128)(2,1)S(1)} %get-tuple-element.12.dq, bf16[128,512]{1,0:T(8,128)(2,1)S(1)} %get-tuple-element.13.dk, bf16[128,512]{1,0:T(8,128)(2,1)S(1)} %get-tuple-element.14.dv, ...), custom_call_target="tpu_custom_call" | custom-call | tf_op jit(solution)/shard_map/write_out/pallas_call | solution.py:549

commit v3 on v2

--- a/solution.py
+++ b/solution.py
@@ -13,6 +13,7 @@
 SOFT = 256
 N_SEQ = 128
 N_DP = 4
+WIDE = 384
 norm_eps = 1e-06
 BF16 = jnp.bfloat16
 F32 = jnp.float32
@@ -60,8 +61,8 @@
     q_hbm, k_hbm, v_hbm, g_hbm, w_hbm, gain_hbm,
     dq_ref, dk_ref, dv_ref, wg_ref,
     q_ref, k_ref, v_ref, g_ref, w_ref, gain_ref,
-    kx, vx, phi_part, phi_turned, term, s_xy, s_z, s_full,
-    w_in, w_rows, w_all, g_in, attn_own, attn_in,
+    kx, vx, phi_part, phi_turned, key_part, slope_keep, term, s_xy, s_z, s_full,
+    w_in, w_rows, w_all, t_in, t_rows, t_all, t_sorted, g_in, attn_own, attn_in,
     probs, u_keep, wg_out, wg_in, wg_zout, wg_zin, wg_sum, wg_fin,
     back_out, back_in, dkv_keep,
     lsem, ssem, rsem,
@@ -82,9 +83,11 @@
         pltpu.make_async_copy(src, dst, lsem.at[i])
         for i, (src, dst) in enumerate(
             (
-                (k_hbm, k_ref),
-                (v_hbm, v_ref),
+                (k_hbm.at[:, pl.ds(SOFT, SOFT)], k_ref.at[:, pl.ds(SOFT, SOFT)]),
+                (v_hbm.at[:, pl.ds(SOFT, SOFT)], v_ref.at[:, pl.ds(SOFT, SOFT)]),
                 (w_hbm, w_ref),
+                (k_hbm.at[:, pl.ds(0, SOFT)], k_ref.at[:, pl.ds(0, SOFT)]),
+                (v_hbm.at[:, pl.ds(0, SOFT)], v_ref.at[:, pl.ds(0, SOFT)]),
                 (q_hbm, q_ref),
                 (gain_hbm, gain_ref),
                 (g_hbm, g_ref),
@@ -256,25 +259,28 @@
     state_sum = Total(
         0,
         [
-            dot_wide(unit_plus(k_ref[:, head(2 + h)].astype(F32)), v_ref[:, head(2 + h)], 0, 0)
+            dot(unit_plus(k_ref[:, head(2 + h)].astype(F32)).astype(BF16), v_ref[:, head(2 + h)], 0, 0)
             for h in range(2)
         ],
     )
     loads[2].wait()
-    w_in[z * 2 + core] = jnp.where(
-        core == 0, w_ref[:, 0:512].astype(F32), w_ref[:, 512:1024].astype(F32)
-    ).astype(BF16)
+    w_piece = jnp.where(core == 0, w_ref[:, 0:512].astype(F32), w_ref[:, 512:1024].astype(F32)).astype(BF16)
+    w_in[z * 2 + core] = w_piece[:, 0:WIDE]
+    t_in[p * 2 + core] = w_piece[:, WIDE:512]
 
     pl.semaphore_wait(barrier, len(peers))
 
     state_sum.start()
-    w_mine = w_hbm.at[:, pl.ds(pl.multiple_of(core * 512, 512), 512)]
-    w_cross = w_hbm.at[:, pl.ds(pl.multiple_of(other * 512, 512), 512)]
+    def w_part(of, first, width):
+        return w_hbm.at[:, pl.ds(pl.multiple_of(of * 512 + first, 128), width)]
+
     w_slot = w_in.at[z * 2 + core]
-    w_copy = [send(w_cross, w_slot, partner)]
+    w_copy = [send(w_part(other, 0, WIDE), w_slot, partner)]
     for d in FAR:
-        w_copy.append(send(w_mine, w_slot, z_peer(d)))
-        w_copy.append(send(w_cross, w_slot, z_cross(d)))
+        w_copy.append(send(w_part(core, 0, WIDE), w_slot, z_peer(d)))
+        w_copy.append(send(w_part(other, 0, WIDE), w_slot, z_cross(d)))
+    t_slot = t_in.at[p * 2 + core]
+    t_copy = [send(w_part((core + cross) % 2, WIDE, 128), t_slot, flat_peer(d, cross)) for d, cross in near]
     soft = pl.ds(0, SOFT)
     k_copy = [
         send(k_hbm.at[:, soft], kx.at[0], after),
@@ -293,9 +299,21 @@
     for h in range(2):
         for i, part in enumerate(parts(unit_plus(q_ref[:, head(2 + h)].astype(F32)))):
             phi_part[h, i] = part
-            phi_turned[h, i] = part.T
+            if i == 0:
+                phi_turned[h] = part.T
+        k_l = k_ref[:, head(2 + h)].astype(F32)
+        slope_keep[h] = unit_slope(k_l)
+        for i, part in enumerate(parts(unit_plus(k_l))):
+            key_part[h, i] = part
 
     state_sum.along_z()
+
+    arrived(t_copy)
+    for i in range(16):
+        t_rows[4 * i : 4 * i + 4, :] = t_in[i].astype(F32)
+    t_all[core, z] = t_rows[...].astype(BF16)
+    t_mine = t_all.at[core, z]
+    t_copy = [send(t_mine, t_mine, z_peer(d)) for d in FAR]
 
     arrived(w_copy)
     for i in range(16):
@@ -353,6 +371,18 @@
         w_copy[d].wait_recv()
         block = w_block((p + 8 - d) % 8)
         w_swap.append(send(block, block, partner))
+    arrived(t_copy)
+    w_swap.append(send(t_all.at[core], t_all.at[core], partner))
+
+    def t_sort(c, groups):
+        for group in groups:
+            for i in range(8):
+                first = group * 64 + i * 8
+                t_sorted[c, first : first + 8, :] = t_all[c, i, group * 8 : group * 8 + 8, :]
+
+    def d_attn_of(c, rows):
+        wide = dot(g_ref[:, c * 512 : c * 512 + WIDE], w_all[c, rows, :], 1, 1)
+        return wide + dot(g_ref[:, c * 512 + WIDE : c * 512 + 512], t_sorted[c, rows, :], 1, 1)
 
     state = state_sum.value()
 
@@ -366,10 +396,10 @@
     lin = pl.ds(SOFT, SOFT)
     a_copy = [send(attn_own.at[:, lin], attn_in.at[:, lin], partner)]
 
-    mine_lin = dot(g_mine, w_all[core, SOFT:512, :], 1, 1)
     arrived(w_swap)
-    g_cross = g_ref[:, pl.ds(pl.multiple_of(other * 512, 512), 512)]
-    d_attn_lin = (mine_lin + dot(g_cross, w_all[other, SOFT:512, :], 1, 1)).astype(BF16)
+    for c in range(2):
+        t_sort(c, range(4, 8))
+    d_attn_lin = (d_attn_of(0, slice(SOFT, 512)) + d_attn_of(1, slice(SOFT, 512))).astype(BF16)
 
     grad_u = []
     for h in range(2):
@@ -379,18 +409,16 @@
         grad_u.append(r * g_lin - u * (r * r * r) * jnp.mean(g_lin * u, axis=1, keepdims=True))
     terms = []
     for h in range(2):
-        high, low = parts(grad_u[h])
-        terms.append(
-            dot(phi_turned[h, 0], high, 1, 0) + dot(phi_turned[h, 0], low, 1, 0) + dot(phi_turned[h, 1], high, 1, 0)
-        )
+        terms.append(dot(phi_turned[h], grad_u[h].astype(BF16), 1, 0))
     grad_sum = Total(1, terms)
     grad_sum.start()
 
     arrived(a_copy)
     wg_lin = Half(1, g_mine, g_in[...])
     wg_lin.xy()
-    d_attn = dot(g_ref[:, 0:512], w_all[0, 0:SOFT, :], 1, 1) + dot(g_ref[:, 512:1024], w_all[1, 0:SOFT, :], 1, 1)
-    d_attn = d_attn.astype(BF16)
+    for c in range(2):
+        t_sort(c, range(4))
+    d_attn = (d_attn_of(0, slice(0, SOFT)) + d_attn_of(1, slice(0, SOFT))).astype(BF16)
     wg_soft.along_z()
 
     for h in range(2):
@@ -440,11 +468,10 @@
     wg_lin.deliver()
     dstate = grad_sum.value()
     for h in range(2):
-        k_l = k_ref[:, head(2 + h)].astype(F32)
-        v_l = v_ref[:, head(2 + h)]
-        dk_lin = dot(v_l, dstate[h], 1, 1) * unit_slope(k_l)
+        dk_lin = dot(v_ref[:, head(2 + h)], dstate[h], 1, 1) * slope_keep[h]
         dk_ref[:, head(2 + h)] = dk_lin.astype(BF16)
-        dv_ref[:, head(2 + h)] = dot_wide(unit_plus(k_l), dstate[h], 1, 0).astype(BF16)
+        dv_lin = dot(key_part[h, 0], dstate[h], 1, 0) + dot(key_part[h, 1], dstate[h], 1, 0)
+        dv_ref[:, head(2 + h)] = dv_lin.astype(BF16)
 
     for step in steps:
         to_dp, flip, cross = step
@@ -471,7 +498,7 @@
 
 N_COPIES = (
     2 * (15 + 7 + 15)
-    + 15 + 7 + 8
+    + 15 + 7 + 8 + 15 + 7 + 1
     + 4 + 1 + 2
     + 2 * (7 + 7)
     + 2
@@ -510,14 +537,20 @@
             pltpu.VMEM((2, ROWS, SOFT), BF16),
             pltpu.VMEM((2, ROWS, SOFT), BF16),
             pltpu.VMEM((2, 2, ROWS, DH), BF16),
-            pltpu.VMEM((2, 2, DH, ROWS), BF16),
+            pltpu.VMEM((2, DH, ROWS), BF16),
+            pltpu.VMEM((2, 2, ROWS, DH), BF16),
+            pltpu.VMEM((2, ROWS, DH), F32),
             pltpu.VMEM((2, 2, 8, 16, DH), BF16),
             pltpu.VMEM((2, 8, 2, 16, DH), BF16),
             pltpu.VMEM((2, 8, 16, DH), BF16),
             pltpu.VMEM((2, 2, 8, 16, DH), BF16),
-            pltpu.VMEM((16, 4, 512), BF16),
-            pltpu.VMEM((64, 512), F32),
-            pltpu.VMEM((2, 512, 512), BF16),
+            pltpu.VMEM((16, 4, WIDE), BF16),
+            pltpu.VMEM((64, WIDE), F32),
+            pltpu.VMEM((2, 512, WIDE), BF16),
+            pltpu.VMEM((16, 4, 128), BF16),
+            pltpu.VMEM((64, 128), F32),
+            pltpu.VMEM((2, 8, 64, 128), BF16),
+            pltpu.VMEM((2, 512, 128), BF16),
             pltpu.VMEM((ROWS, 512), BF16),
             pltpu.VMEM((ROWS, 512), BF16),
             pltpu.VMEM((ROWS, 512), BF16),
@@ -532,7 +565,7 @@
             pltpu.VMEM((2, 2, ROWS, SOFT), BF16),
             pltpu.VMEM((2, 2, ROWS, SOFT), BF16),
             pltpu.VMEM((2, ROWS, SOFT), F32),
-            pltpu.SemaphoreType.DMA((6,)),
+            pltpu.SemaphoreType.DMA((8,)),
             pltpu.SemaphoreType.DMA((N_COPIES + 16,)),
             pltpu.SemaphoreType.DMA((N_COPIES + 16,)),
         ],

time: 51.8 us -> 51.1 us (0.986)
  Pallas kernels: 51 us -> 50.3 us
    pallas_call x1, Pallas kernels: 50.2 us -> 49.5 us  [body(): pl.pallas_call(kernel, out_shape=tuple((pltpu.VMEM(*result) for result in...]
where the time goes in v3:
time: 51.1 us; the launch traced here: 50.9 us
  Pallas kernels  50.3 us (98%)
  between operations  0.64 us (1%)
    pallas_call x1, Pallas kernels, body(): pl.pallas_call(kernel, out_shape=tuple((pltpu.VMEM(*result) for result in...  49.5 us

profile of v3, /device:TPU:9, one launch (start us, length us, event | category | flops | bytes accessed | tf_op | source)
XLA Modules:
  0.0 50.9 jit_solution(11478748874622710960)
XLA Ops:
  0.6 49.5 %sublayer_backward.1 = (bf16[128,512]{1,0:T(8,128)(2,1)S(1)}, bf16[128,512]{1,0:T(8,128)(2,1)S(1)}, bf16[128,512]{1,0:T(8,128)(2,1)S(1)}, f32[4,1024]{1,0:T(4,128)S(1)}) custom-call(bf16[128,512]{1,0:T(8,128)(2,1)} %bitcast.9, bf16[128,512]{1,0:T(8,128)(2,1)} %bitcast.10, bf16[128,512]{1,0:T(8,128)(2,1)} %bitcast.11, bf16[128,1024]{1,0:T(8,128)(2,1)} %bitcast.8, ...), custom_call_target="tpu_custom_call" | custom-call | tf_op jit(solution)/shard_map/sublayer_backward/pallas_call | solution.py:525
  50.2 0.8 %write_out.1 = (bf16[128,512]{1,0:T(8,128)(2,1)}, bf16[128,512]{1,0:T(8,128)(2,1)}, bf16[128,512]{1,0:T(8,128)(2,1)}, f32[4,1024]{1,0:T(4,128)}) custom-call(bf16[128,512]{1,0:T(8,128)(2,1)S(1)} %get-tuple-element.12.dq, bf16[128,512]{1,0:T(8,128)(2,1)S(1)} %get-tuple-element.13.dk, bf16[128,512]{1,0:T(8,128)(2,1)S(1)} %get-tuple-element.14.dv, ...), custom_call_target="tpu_custom_call" | custom-call | tf_op jit(solution)/shard_map/write_out/pallas_call | solution.py:582

commit v4 on v3

--- a/solution.py
+++ b/solution.py
@@ -188,12 +188,17 @@
             return [s_full[self.i, h].reshape(DH, DH) for h in range(2)]
 
     class Half:
-        def __init__(self, half, g_mine, g_other):
+        def __init__(self, half, g_mine):
             self.s = s = half
+            self.own = [dot(attn_own[:, self.rows(b)], g_mine, 0, 0) for b in range(4)]
+
+        def rows(self, b):
+            return slice(self.s * SOFT + b * 64, self.s * SOFT + (b + 1) * 64)
+
+        def join(self, g_other):
+            s = self.s
             for b in range(4):
-                rows = slice(s * SOFT + b * 64, s * SOFT + (b + 1) * 64)
-                block = dot(attn_own[:, rows], g_mine, 0, 0) + dot(attn_in[:, rows], g_other, 0, 0)
-                block = block.astype(BF16)
+                block = (self.own[b] + dot(attn_in[:, self.rows(b)], g_other, 0, 0)).astype(BF16)
                 wg_out[s, b] = block[:, 0:256]
                 wg_out[s, 4 + b] = block[:, 256:512]
 
@@ -217,7 +222,7 @@
             for d in range(1, 8):
                 total = total + wg_zin[s, d].astype(F32)
             for c in range(2):
-                wg_sum[s, c] = total[4 * c : 4 * c + 4]
+                wg_sum[s, c] = total[4 * c : 4 * c + 4].astype(BF16)
             flip = (s + y) % 2
             owner = ((s * 4 + p % 4) * 8 + z) * 2
 
@@ -361,10 +366,11 @@
 
     state_sum.spread()
 
+    g_mine = g_ref[:, pl.ds(pl.multiple_of(core * 512, 512), 512)]
+    wg_soft = Half(0, g_mine)
     arrived(g_copy)
     arrived(a_copy)
-    g_mine = g_ref[:, pl.ds(pl.multiple_of(core * 512, 512), 512)]
-    wg_soft = Half(0, g_mine, g_in[...])
+    wg_soft.join(g_in[...])
     wg_soft.xy()
 
     for d in FAR[::-1]:
@@ -381,8 +387,12 @@
                 t_sorted[c, first : first + 8, :] = t_all[c, i, group * 8 : group * 8 + 8, :]
 
     def d_attn_of(c, rows):
-        wide = dot(g_ref[:, c * 512 : c * 512 + WIDE], w_all[c, rows, :], 1, 1)
-        return wide + dot(g_ref[:, c * 512 + WIDE : c * 512 + 512], t_sorted[c, rows, :], 1, 1)
+        g_wide = g_ref[:, pl.ds(pl.multiple_of(c * 512, 128), WIDE)]
+        g_rest = g_ref[:, pl.ds(pl.multiple_of(c * 512 + WIDE, 128), 128)]
+        return dot(g_wide, w_all[c, rows, :], 1, 1) + dot(g_rest, t_sorted[c, rows, :], 1, 1)
+
+    t_sort(core, range(4, 8))
+    mine_lin = d_attn_of(core, slice(SOFT, 512))
 
     state = state_sum.value()
 
@@ -397,9 +407,8 @@
     a_copy = [send(attn_own.at[:, lin], attn_in.at[:, lin], partner)]
 
     arrived(w_swap)
-    for c in range(2):
-        t_sort(c, range(4, 8))
-    d_attn_lin = (d_attn_of(0, slice(SOFT, 512)) + d_attn_of(1, slice(SOFT, 512))).astype(BF16)
+    t_sort(other, range(4, 8))
+    d_attn_lin = (mine_lin + d_attn_of(other, slice(SOFT, 512))).astype(BF16)
 
     grad_u = []
     for h in range(2):
@@ -412,10 +421,11 @@
         terms.append(dot(phi_turned[h], grad_u[h].astype(BF16), 1, 0))
     grad_sum = Total(1, terms)
     grad_sum.start()
-
+    wg_lin = Half(1, g_mine)
     arrived(a_copy)
-    wg_lin = Half(1, g_mine, g_in[...])
+    wg_lin.join(g_in[...])
     wg_lin.xy()
+
     for c in range(2):
         t_sort(c, range(4))
     d_attn = (d_attn_of(0, slice(0, SOFT)) + d_attn_of(1, slice(0, SOFT))).astype(BF16)
@@ -486,7 +496,8 @@
         ).wait_recv()
     for c in range(2):
         for half in range(2):
-            total = (wg_fin[0, c, half] + wg_fin[1, c, half]) + (wg_fin[2, c, half] + wg_fin[3, c, half])
+            shares = [wg_fin[i, c, half].astype(F32) for i in range(N_DP)]
+            total = (shares[0] + shares[1]) + (shares[2] + shares[3])
             first = c * 512 + half * 256
             wg_ref[:, first : first + 256] = total * (1.0 / math.sqrt(N_DP * N_SEQ * ROWS))
     wg_soft.finish()
@@ -560,8 +571,8 @@
             pltpu.VMEM((2, 8, 64, 256), BF16),
             pltpu.VMEM((2, 8, 8, 256), BF16),
             pltpu.VMEM((2, 8, 8, 256), BF16),
-            pltpu.VMEM((2, 2, 4, 256), F32),
-            pltpu.VMEM((N_DP, 2, 2, 4, 256), F32),
+            pltpu.VMEM((2, 2, 4, 256), BF16),
+            pltpu.VMEM((N_DP, 2, 2, 4, 256), BF16),
             pltpu.VMEM((2, 2, ROWS, SOFT), BF16),
             pltpu.VMEM((2, 2, ROWS, SOFT), BF16),
             pltpu.VMEM((2, ROWS, SOFT), F32),

time: 51.1 us -> 51 us (level)
  no operation moved by 1% of the time
where the time goes in v4:
time: 51 us; the launch traced here: 50.8 us
  Pallas kernels  50.2 us (98%)
  between operations  0.64 us (1%)
    pallas_call x1, Pallas kernels, body(): pl.pallas_call(kernel, out_shape=tuple((pltpu.VMEM(*result) for result in...  49.4 us

profile of v4, /device:TPU:9, one launch (start us, length us, event | category | flops | bytes accessed | tf_op | source)
XLA Modules:
  0.0 50.8 jit_solution(12922115700595381723)
XLA Ops:
  0.6 49.4 %sublayer_backward.1 = (bf16[128,512]{1,0:T(8,128)(2,1)S(1)}, bf16[128,512]{1,0:T(8,128)(2,1)S(1)}, bf16[128,512]{1,0:T(8,128)(2,1)S(1)}, f32[4,1024]{1,0:T(4,128)S(1)}) custom-call(bf16[128,512]{1,0:T(8,128)(2,1)} %bitcast.9, bf16[128,512]{1,0:T(8,128)(2,1)} %bitcast.10, bf16[128,512]{1,0:T(8,128)(2,1)} %bitcast.11, bf16[128,1024]{1,0:T(8,128)(2,1)} %bitcast.8, ...), custom_call_target="tpu_custom_call" | custom-call | tf_op jit(solution)/shard_map/sublayer_backward/pallas_call | solution.py:536
  50.1 0.8 %write_out.1 = (bf16[128,512]{1,0:T(8,128)(2,1)}, bf16[128,512]{1,0:T(8,128)(2,1)}, bf16[128,512]{1,0:T(8,128)(2,1)}, f32[4,1024]{1,0:T(4,128)}) custom-call(bf16[128,512]{1,0:T(8,128)(2,1)S(1)} %get-tuple-element.12.dq, bf16[128,512]{1,0:T(8,128)(2,1)S(1)} %get-tuple-element.13.dk, bf16[128,512]{1,0:T(8,128)(2,1)S(1)} %get-tuple-element.14.dv, ...), custom_call_target="tpu_custom_call" | custom-call | tf_op jit(solution)/shard_map/write_out/pallas_call | solution.py:593

commit v5 on v4

--- a/solution.py
+++ b/solution.py
@@ -222,7 +222,7 @@
             for d in range(1, 8):
                 total = total + wg_zin[s, d].astype(F32)
             for c in range(2):
-                wg_sum[s, c] = total[4 * c : 4 * c + 4].astype(BF16)
+                wg_sum[s, c] = total[4 * c : 4 * c + 4]
             flip = (s + y) % 2
             owner = ((s * 4 + p % 4) * 8 + z) * 2
 
@@ -406,6 +406,9 @@
     lin = pl.ds(SOFT, SOFT)
     a_copy = [send(attn_own.at[:, lin], attn_in.at[:, lin], partner)]
 
+    wg_lin = Half(1, g_mine)
+    arrived(a_copy)
+    wg_lin.join(g_in[...])
     arrived(w_swap)
     t_sort(other, range(4, 8))
     d_attn_lin = (mine_lin + d_attn_of(other, slice(SOFT, 512))).astype(BF16)
@@ -421,9 +424,6 @@
         terms.append(dot(phi_turned[h], grad_u[h].astype(BF16), 1, 0))
     grad_sum = Total(1, terms)
     grad_sum.start()
-    wg_lin = Half(1, g_mine)
-    arrived(a_copy)
-    wg_lin.join(g_in[...])
     wg_lin.xy()
 
     for c in range(2):
@@ -496,8 +496,7 @@
         ).wait_recv()
     for c in range(2):
         for half in range(2):
-            shares = [wg_fin[i, c, half].astype(F32) for i in range(N_DP)]
-            total = (shares[0] + shares[1]) + (shares[2] + shares[3])
+            total = (wg_fin[0, c, half] + wg_fin[1, c, half]) + (wg_fin[2, c, half] + wg_fin[3, c, half])
             first = c * 512 + half * 256
             wg_ref[:, first : first + 256] = total * (1.0 / math.sqrt(N_DP * N_SEQ * ROWS))
     wg_soft.finish()
@@ -571,8 +570,8 @@
             pltpu.VMEM((2, 8, 64, 256), BF16),
             pltpu.VMEM((2, 8, 8, 256), BF16),
             pltpu.VMEM((2, 8, 8, 256), BF16),
-            pltpu.VMEM((2, 2, 4, 256), BF16),
-            pltpu.VMEM((N_DP, 2, 2, 4, 256), BF16),
+            pltpu.VMEM((2, 2, 4, 256), F32),
+            pltpu.VMEM((N_DP, 2, 2, 4, 256), F32),
             pltpu.VMEM((2, 2, ROWS, SOFT), BF16),
             pltpu.VMEM((2, 2, ROWS, SOFT), BF16),
             pltpu.VMEM((2, ROWS, SOFT), F32),

time: 51 us -> 52 us (1.020)
  Pallas kernels: 50.2 us -> 51.3 us
    pallas_call x1, Pallas kernels: 49.4 us -> 50.5 us  [body(): pl.pallas_call(kernel, out_shape=tuple((pltpu.VMEM(*result) for result in...]
where the time goes in v5:
time: 52 us; the launch traced here: 51.9 us
  Pallas kernels  51.3 us (99%)
  between operations  0.64 us (1%)
    pallas_call x1, Pallas kernels, body(): pl.pallas_call(kernel, out_shape=tuple((pltpu.VMEM(*result) for result in...  50.5 us

profile of v5, /device:TPU:9, one launch (start us, length us, event | category | flops | bytes accessed | tf_op | source)
XLA Modules:
  0.0 51.9 jit_solution(15359454537255250193)
XLA Ops:
  0.6 50.5 %sublayer_backward.1 = (bf16[128,512]{1,0:T(8,128)(2,1)S(1)}, bf16[128,512]{1,0:T(8,128)(2,1)S(1)}, bf16[128,512]{1,0:T(8,128)(2,1)S(1)}, f32[4,1024]{1,0:T(4,128)S(1)}) custom-call(bf16[128,512]{1,0:T(8,128)(2,1)} %bitcast.9, bf16[128,512]{1,0:T(8,128)(2,1)} %bitcast.10, bf16[128,512]{1,0:T(8,128)(2,1)} %bitcast.11, bf16[128,1024]{1,0:T(8,128)(2,1)} %bitcast.8, ...), custom_call_target="tpu_custom_call" | custom-call | tf_op jit(solution)/shard_map/sublayer_backward/pallas_call | solution.py:535
  51.1 0.8 %write_out.1 = (bf16[128,512]{1,0:T(8,128)(2,1)}, bf16[128,512]{1,0:T(8,128)(2,1)}, bf16[128,512]{1,0:T(8,128)(2,1)}, f32[4,1024]{1,0:T(4,128)}) custom-call(bf16[128,512]{1,0:T(8,128)(2,1)S(1)} %get-tuple-element.12.dq, bf16[128,512]{1,0:T(8,128)(2,1)S(1)} %get-tuple-element.13.dk, bf16[128,512]{1,0:T(8,128)(2,1)S(1)} %get-tuple-element.14.dv, ...), custom_call_target="tpu_custom_call" | custom-call | tf_op jit(solution)/shard_map/write_out/pallas_call | solution.py:592
